TPU v7x, 256 devices: a whole 4x4x8 slice. The times are simulated.
256 devices in a mesh: fsdp: 16 (over y, z_hi), seq: 16 (over x, z_lo, core).
Axes of the slice: x: 4, y: 4, z: 8 (z_hi: 4, z_lo: 2; z = z_hi * 2 + z_lo), core: 2. Of those that a mesh axis runs over, the one named last changes fastest.
Arguments:
- hidden: bfloat16 [16, 2048, 5120], P('fsdp', 'seq'), may hold values from -6 to 6
- queries: bfloat16 [16, 2048, 4096], P('fsdp', 'seq'), may hold values from -400 to 400
- key_value_weight: bfloat16 [5120, 2048], P('fsdp'), may hold values from -0.078125 to 0.078125
- doc_lengths: int32 [16, 16], P('fsdp'), may hold values from 1 to 1024, 2048 in all within a row
- resp_lengths: int32 [16, 16], P('fsdp'), may hold values from 1 to 128
Outputs:
- attended: bfloat16 [16, 2048, 4096], P('fsdp', 'seq')
- pooled: float32 [16, 16, 4096], P('fsdp', None, 'seq')
Inputs may be any that keep to these rules, and one draw needn't show every extreme that they name: `doc_lengths`: each row holds the lengths of the documents of one packed sequence in order; they sum to 2048 and the longest is exactly 1024.
All inputs are finite; a program needn't handle non-finite values.
Results may differ from a plain program's by a relative error of at most 0.011.
Values may be sent and summed in bfloat16 or wider, within the bound.
No kernel may reach another device: no remote copies, remote signals or barrier semaphores. Data moves between devices by JAX's collectives and lax.ppermute only.
A program may use at most 128 MiB of HBM per device.

v0:
```python
import jax
import jax.numpy as jnp
from jax import lax
from jax.sharding import PartitionSpec as P

HEAD_SIZE = 128
KEY_VALUE_HEADS = 8
ROPE_BASE = 1000000.0


def token_tables(lengths, wanted, first, count):
    ends = jnp.cumsum(lengths)
    starts = ends - lengths
    answer = jnp.minimum(wanted, lengths)
    index = first + jnp.arange(count, dtype=jnp.int32)
    inside = (index[:, None] >= starts[None, :]) & (index[:, None] < ends[None, :])
    token_position = jnp.sum(jnp.where(inside, index[:, None] - starts[None, :], 0), axis=1)
    doc_id = jnp.sum(jnp.where(index[:, None] >= ends[None, :], 1, 0), axis=1).astype(jnp.int32)
    member = jnp.where(inside & (index[:, None] >= (ends - answer)[None, :]), 1, 0).astype(
        jnp.int32
    )
    return (token_position, doc_id, member, answer)


def rotate_pairs(heads, token_position):
    half = heads.shape[-1] // 2
    freq = ROPE_BASE ** (-(jnp.arange(half, dtype=jnp.float32) * 2.0 / heads.shape[-1]))
    angle = token_position.astype(jnp.float32)[:, None] * freq[None, :]
    cosine = jnp.cos(angle)[:, None, :]
    sine = jnp.sin(angle)[:, None, :]
    first = heads[..., :half]
    second = heads[..., half:]
    return jnp.concatenate(
        [first * cosine - second * sine, second * cosine + first * sine], axis=-1
    )


def on_device(hidden, queries, key_value_weight, doc_lengths, resp_lengths):
    piece_list = lax.axis_size("seq")
    rank = lax.axis_index("seq")
    token_batch = hidden.shape[1]
    length = token_batch * piece_list
    longest = length // 2
    kv_cols = key_value_weight.shape[1]
    key_value_split = kv_cols // 2
    lengths = doc_lengths[0]
    wanted = resp_lengths[0]
    features = hidden[0]
    projected_rows = jnp.dot(
        features,
        lax.all_gather(key_value_weight, "fsdp", axis=0, tiled=True),
        preferred_element_type=jnp.float32,
    )
    local_tables = token_tables(lengths, wanted, rank * token_batch, token_batch)
    key_rows = rotate_pairs(
        projected_rows[:, :key_value_split].reshape(token_batch, KEY_VALUE_HEADS, HEAD_SIZE),
        local_tables[0],
    ).astype(jnp.bfloat16)
    value_rows = (
        projected_rows[:, key_value_split:]
        .reshape(token_batch, KEY_VALUE_HEADS, HEAD_SIZE)
        .astype(jnp.bfloat16)
    )
    repeat_heads = max(1, piece_list // KEY_VALUE_HEADS)
    key_rows = jnp.broadcast_to(
        key_rows[:, :, None, :], (token_batch, KEY_VALUE_HEADS, repeat_heads, HEAD_SIZE)
    ).reshape(1, token_batch, KEY_VALUE_HEADS * repeat_heads * HEAD_SIZE)
    value_rows = jnp.broadcast_to(
        value_rows[:, :, None, :], (token_batch, KEY_VALUE_HEADS, repeat_heads, HEAD_SIZE)
    ).reshape(1, token_batch, KEY_VALUE_HEADS * repeat_heads * HEAD_SIZE)
    q_heads, k_heads, v_heads = (
        lax.all_to_all(queries, "seq", split_axis=2, concat_axis=1, tiled=True),
        lax.all_to_all(key_rows, "seq", split_axis=2, concat_axis=1, tiled=True),
        lax.all_to_all(value_rows, "seq", split_axis=2, concat_axis=1, tiled=True),
    )
    q_count = q_heads.shape[2] // HEAD_SIZE
    kv_count = k_heads.shape[2] // HEAD_SIZE
    query_group = q_count // kv_count
    all_tables = token_tables(lengths, wanted, jnp.int32(0), length)
    doc_id = all_tables[1]
    answer = all_tables[3]
    query_matrix = q_heads[0].reshape(length, kv_count, query_group, HEAD_SIZE)
    key_all = k_heads[0].reshape(length, kv_count, HEAD_SIZE)
    value_all = v_heads[0].reshape(length, kv_count, HEAD_SIZE)
    block = min(512, length)
    window = min(length, block + longest)

    def attend(index):
        qstart = index * block
        kstart = jnp.maximum(qstart + block - window, 0)
        qblock = lax.dynamic_slice_in_dim(query_matrix, qstart, block, 0)
        kblock = lax.dynamic_slice_in_dim(key_all, kstart, window, 0)
        vblock = lax.dynamic_slice_in_dim(value_all, kstart, window, 0)
        qdoc = lax.dynamic_slice_in_dim(doc_id, qstart, block, 0)
        kdoc = lax.dynamic_slice_in_dim(doc_id, kstart, window, 0)
        qplace = qstart + jnp.arange(block, dtype=jnp.int32)
        kplace = kstart + jnp.arange(window, dtype=jnp.int32)
        allowed = (qdoc[:, None] == kdoc[None, :]) & (kplace[None, :] <= qplace[:, None])
        scores = jnp.einsum(
            "qkgd,skd->kgqs", qblock, kblock, preferred_element_type=jnp.float32
        ) * HEAD_SIZE ** (-0.5)
        scores = jnp.where(allowed, scores, -1e30)
        peak = jnp.max(scores, axis=-1, keepdims=True)
        weight = jnp.where(allowed, jnp.exp(scores - peak), 0.0)
        probs = (weight / jnp.sum(weight, axis=-1, keepdims=True)).astype(jnp.bfloat16)
        output = jnp.einsum("kgqs,skd->qkgd", probs, vblock, preferred_element_type=jnp.float32)
        return output.astype(jnp.bfloat16).reshape(block, q_count * HEAD_SIZE)

    attn_heads = lax.map(attend, jnp.arange(length // block, dtype=jnp.int32)).reshape(
        length, q_count * HEAD_SIZE
    )
    attended = lax.all_to_all(attn_heads[None], "seq", split_axis=1, concat_axis=2, tiled=True)
    partial_value = jnp.einsum(
        "tr,tc->rc",
        local_tables[2].astype(jnp.bfloat16),
        attended[0],
        preferred_element_type=jnp.float32,
    )
    sums = lax.psum_scatter(
        partial_value.astype(jnp.bfloat16), "seq", scatter_dimension=1, tiled=True
    ).astype(jnp.float32)
    pooled = sums / answer.astype(jnp.float32)[:, None]
    return (attended, pooled[None])


def solution(mesh):
    in_specs = (
        P("fsdp", "seq", None),
        P("fsdp", "seq", None),
        P("fsdp", None),
        P("fsdp", None),
        P("fsdp", None),
    )
    out_specs = (P("fsdp", "seq", None), P("fsdp", None, "seq"))
    return jax.shard_map(
        on_device, mesh=mesh, in_specs=in_specs, out_specs=out_specs, check_vma=False
    )
```

profile of v0, /device:TPU:8, one launch (start us, length us, event | category | flops | bytes accessed | tf_op | source)
XLA Modules:
  0.0 494.3 jit_solution(4194151677751714912)
XLA Ops:
  7.9 5.0 %copy.69 = bf16[1,128,4096]{1,0,2:T(2,128)(2,1)S(1)} copy(bf16[1,128,4096]{2,1,0:T(8,128)(2,1)} %param.8) | data formatting | bytes 2097152 | tf_op args[1]
  13.5 23.4 %reduce.18 = bf16[4096,128]{1,0:T(8,128)(2,1)} reduce(bf16[4096,1,128]{2,1,0:T(2,128)(2,1)S(1)} %bitcast.129, bf16[]{:T(256)} %broadcast.95), dimensions={1}, to_apply=%bitcast.91.reduce_sub_computation | reduce | bytes 2097154
  39.0 6.2 %all-to-all-start.2 = ((bf16[16,2,16384]{2,1,0:T(2,128)(2,1)}), bf16[16,2,16384]{2,1,0:T(2,128)(2,1)S(1)}, u32[]{:S(2)}, u32[]{:S(2)}) async-start(bf16[16,2,16384]{2,1,0:T(2,128)(2,1)} %reshape.212), calls=%async_computation.2 | async-start | bytes 2097152 | tf_op jit(solution)/shard_map/all_to_all | solution.py:72
  46.5 221.5 %all-gather.2.cloned.1.call-done = bf16[5120,2048]{1,0:T(8,128)(2,1)} async-done(((bf16[320,2048]{1,0:T(8,128)(2,1)}), bf16[5120,2048]{1,0:T(8,128)(2,1)}) %all-gather.2.cloned.1.call-update) | async-done | bytes 20971536 | tf_op jit(solution)/shard_map/all_gather | solution.py:51
  268.0 8.5 %fusion.19 = f32[128,2048]{1,0:T(8,128)S(1)} fusion(bf16[5120,2048]{1,0:T(8,128)(2,1)} %all-gather.2.cloned.1.call-done, bf16[1,128,5120]{2,1,0:T(8,128)(2,1)S(1)} %copy-done), kind=kOutput, calls=%fused_computation.25 | convolution fusion | flops 2684354560 | bytes 23330816 | tf_op jit(solution)/shard_map/dot_general | solution.py:49
  277.4 8.1 %copy.93 = bf16[1,128,2048]{1,0,2:T(2,128)(2,1)S(1)} copy(bf16[1,128,2048]{1,2,0:T(8,128)(2,1)S(1)} %bitcast.139) | data formatting | bytes 1048576 | tf_op jit(solution)/shard_map/reshape | solution.py:67
  285.6 12.3 %reduce.17 = bf16[2048,128]{1,0:T(8,128)(2,1)} reduce(bf16[2048,1,128]{2,1,0:T(2,128)(2,1)S(1)} %bitcast.137, bf16[]{:T(256)} %broadcast.95), dimensions={1}, to_apply=%bitcast.105.reduce_sub_computation | reduce | bytes 1048578
  299.8 4.4 all-to-all-start.1
  304.6 8.1 %copy.94 = bf16[1,128,2048]{1,0,2:T(2,128)(2,1)S(1)} copy(bf16[1,128,2048]{1,2,0:T(8,128)(2,1)S(1)} %bitcast.140) | data formatting | bytes 1048576 | tf_op jit(solution)/shard_map/reshape | solution.py:70
  312.7 11.5 %reduce.16 = bf16[2048,128]{1,0:T(8,128)(2,1)S(1)} reduce(bf16[2048,1,128]{2,1,0:T(2,128)(2,1)S(1)} %bitcast.138, bf16[]{:T(256)} %broadcast.95), dimensions={1}, to_apply=%bitcast.106.reduce_sub_computation | reduce | bytes 1048578
  325.2 5.6 %all-to-all-start = ((bf16[16,2,8192]{2,1,0:T(2,128)(2,1)}), bf16[16,2,8192]{2,1,0:T(2,128)(2,1)}, u32[]{:S(2)}, u32[]{:S(2)}) async-start(bf16[16,2,8192]{2,1,0:T(2,128)(2,1)} %reshape.208), calls=%async_computation | async-start | bytes 1048576 | tf_op jit(solution)/shard_map/all_to_all | solution.py:74
  331.2 4.3 reshape.213
  345.0 37.6 %while.14 = (s32[]{:T(128)}, bf16[4,512,256]{2,1,0:T(8,128)(2,1)S(1)}, s32[4]{0:T(128)S(1)}, bf16[2048,1,128]{2,0,1:T(8,128)(2,1)}, s32[2048]{0:T(1024)S(1)}, /*...) while((s32[]{:T(128)}, ...), condition=%wide.region_6.7_spmd, body=%wide.region_3.6_spmd.sunk | while | flops 829816832 | bytes 26538252 | solution.py:109
  347.6 2.5 fusion.40
  357.0 2.5 fusion.40
  361.2 2.4 fusion.42
  366.4 2.5 fusion.40
  370.6 2.4 fusion.42
  375.8 2.5 fusion.40
  383.6 3.2 copy.92
  386.8 10.6 %reduce.19 = bf16[2048,256]{1,0:T(8,128)(2,1)S(1)} reduce(bf16[2048,1,256]{2,1,0:T(2,128)(2,1)S(1)} %bitcast.130, bf16[]{:T(256)} %broadcast.95), dimensions={1}, to_apply=%bitcast.104.reduce_sub_computation | reduce | bytes 2097154
  397.6 20.7 %all_to_all.63 = bf16[16,2,16384]{2,1,0:T(2,128)(2,1)} all-to-all(bf16[16,2,16384]{2,1,0:T(2,128)(2,1)S(1)} %reshape.214), channel_id=1, replica_groups=mesh['fsdp'=16,'seq'=16] {'seq'}, dimensions={0} | all-to-all | bytes 2097152 | tf_op jit(solution)/shard_map/all_to_all | solution.py:112
  418.4 4.3 reshape.215
  427.8 58.0 %reduce-scatter.2.cloned.1.call-done = bf16[16,256]{1,0:T(8,128)(2,1)} async-done(((bf16[16,4096]{1,0:T(8,128)(2,1)}), bf16[16,256]{1,0:T(8,128)(2,1)}) %reduce-scatter.2.cloned.1.call-update) | async-done | bytes 8208 | tf_op jit(solution)/shard_map/reduce_scatter | solution.py:119
  (109 shorter events, 46.2 us)
Async XLA Ops:
  7.2 260.8 %copy-start = (bf16[1,128,5120]{2,1,0:T(8,128)(2,1)S(1)}, bf16[1,128,5120]{2,1,0:T(8,128)(2,1)}, u32[]{:S(2)}) copy-start(bf16[1,128,5120]{2,1,0:T(8,128)(2,1)} %param.7) | copy-start | bytes 3932164
  7.2 38.1 %copy-start.6 = (s32[1,16]{1,0:T(1,128)S(1)}, s32[1,16]{1,0:T(1,128)}, u32[]{:S(2)}) copy-start(s32[1,16]{1,0:T(1,128)} %param.10) | copy-start | bytes 196
  7.2 38.3 %copy-start.8 = (s32[1,16]{1,0:T(1,128)S(1)}, s32[1,16]{1,0:T(1,128)}, u32[]{:S(2)}) copy-start(s32[1,16]{1,0:T(1,128)} %param.11) | copy-start | bytes 196
  7.2 260.8 %all-gather.2.cloned.1.call-start = ((), (), s32[]{:S(2)}) async-start(), calls=%async_computation.5 | async-start | bytes 22282240 | tf_op jit(solution)/shard_map/all_gather | solution.py:51
  39.0 260.8 %all-to-all-start.2 = ((bf16[16,2,16384]{2,1,0:T(2,128)(2,1)}), bf16[16,2,16384]{2,1,0:T(2,128)(2,1)S(1)}, u32[]{:S(2)}, u32[]{:S(2)}) async-start(bf16[16,2,16384]{2,1,0:T(2,128)(2,1)} %reshape.212), calls=%async_computation.2 | async-start | bytes 2097152 | tf_op jit(solution)/shard_map/all_to_all | solution.py:72
  299.8 31.3 %copy-start.2 = (bf16[16,2,16384]{2,1,0:T(2,128)(2,1)}, bf16[16,2,16384]{2,1,0:T(2,128)(2,1)S(1)}, u32[]{:S(2)}) copy-start(bf16[16,2,16384]{2,1,0:T(2,128)(2,1)S(1)} %all-to-all-done.2) | copy-start | bytes 3145732
  299.8 25.3 %all-to-all-start.1 = ((bf16[16,2,8192]{2,1,0:T(2,128)(2,1)}), bf16[16,2,8192]{2,1,0:T(2,128)(2,1)}, u32[]{:S(2)}, u32[]{:S(2)}) async-start(bf16[16,2,8192]{2,1,0:T(2,128)(2,1)} %reshape.210), calls=%async_computation.1 | async-start | bytes 1048576 | tf_op jit(solution)/shard_map/all_to_all | solution.py:73
  325.2 16.5 %all-to-all-start = ((bf16[16,2,8192]{2,1,0:T(2,128)(2,1)}), bf16[16,2,8192]{2,1,0:T(2,128)(2,1)}, u32[]{:S(2)}, u32[]{:S(2)}) async-start(bf16[16,2,8192]{2,1,0:T(2,128)(2,1)} %reshape.208), calls=%async_computation | async-start | bytes 1048576 | tf_op jit(solution)/shard_map/all_to_all | solution.py:74
  330.8 155.1 %reduce-scatter.2.cloned.1.call-start = ((), (), s32[]{:S(2)}) async-start(), calls=%async_computation.6 | async-start | bytes 139264 | tf_op jit(solution)/shard_map/reduce_scatter | solution.py:119
  335.6 9.4 %copy-start.3 = (bf16[4,512,256]{2,1,0:T(8,128)(2,1)S(1)}, bf16[4,512,256]{2,1,0:T(8,128)(2,1)}, u32[]{:S(2)}) copy-start(bf16[4,512,256]{2,1,0:T(8,128)(2,1)} %custom-call) | copy-start | bytes 3145732
  347.6 4.2 copy-start.5
  357.0 4.2 copy-start.5
  366.4 4.2 copy-start.5
  375.8 4.2 copy-start.5
  382.6 1.0 copy-start.4
  397.6 89.6 %copy-start.1 = (bf16[1,128,5120]{2,1,0:T(8,128)(2,1)S(1)}, bf16[1,128,5120]{2,1,0:T(8,128)(2,1)}, u32[]{:S(2)}) copy-start(bf16[1,128,5120]{2,1,0:T(8,128)(2,1)} %param.7) | copy-start | bytes 3932164
  418.4 67.5 %copy-start.7 = (f32[16]{0:T(128)S(1)}, f32[16]{0:T(128)}, u32[]{:S(2)}) copy-start(f32[16]{0:T(128)} %get-tuple-element.205) | copy-start | bytes 196
Sparse Core Ops, SparseCore 0:
  10.5 257.4 all-gather.1
  426.6 59.1 reduce-scatter.1
where the time goes:
time: 500 us; the launch traced here: 494 us
  waiting for transfers between devices  282 us (56%)
  other arithmetic  72.2 us (14%)
  local copies, waits for them, and re-layouts  56.5 us (11%)
  matrix products  29.2 us (6%)
  blocking collectives  20.7 us (4%)
  starting transfers between devices  16.6 us (3%)
  between operations  14.6 us (3%)
    all_gather x1, waiting for transfers between devices, on_device(): lax.all_gather(key_value_weight, 'fsdp', axis=0, tiled=True)  221 us
    reduce_scatter x1, waiting for transfers between devices, on_device(): lax.psum_scatter(partial_value.astype(jnp.bfloat16), 'seq', scatter_dimen...  58 us
    unnamed x4, other arithmetic  57.8 us
    unnamed x33, local copies, waits for them, and re-layouts  27.8 us
    all_to_all x1, blocking collectives, on_device(): lax.all_to_all(attn_heads[None], 'seq', split_axis=1, concat_axis=2, tile...  20.7 us
  transfers between devices with their start and end apart: 5, of which 3 were waited for; matrix products, arithmetic and copies ran while one was open for 19% of the time, Pallas kernels for 0%

commit v1 on v0

--- a/solution.py
+++ b/solution.py
@@ -1,3 +1,4 @@
+import functools
 import jax
 import jax.numpy as jnp
 from jax import lax
@@ -6,6 +7,14 @@
 HEAD_SIZE = 128
 KEY_VALUE_HEADS = 8
 ROPE_BASE = 1000000.0
+
+
+def _recast_tracks(arr_in, mesh_ax):
+    wide_out = jax.lax.all_to_all(jnp.stack(jax.lax.axis_size(mesh_ax) * [arr_in]), mesh_ax, 0, 0)
+    return jnp.concatenate(wide_out, axis=0)
+
+
+expand_the_bars = functools.partial(_recast_tracks, mesh_ax="fsdp")
 
 
 def token_tables(lengths, wanted, first, count):
@@ -47,9 +56,7 @@
     wanted = resp_lengths[0]
     features = hidden[0]
     projected_rows = jnp.dot(
-        features,
-        lax.all_gather(key_value_weight, "fsdp", axis=0, tiled=True),
-        preferred_element_type=jnp.float32,
+        features, expand_the_bars(key_value_weight), preferred_element_type=jnp.float32
     )
     local_tables = token_tables(lengths, wanted, rank * token_batch, token_batch)
     key_rows = rotate_pairs(

time: 500 us -> 770 us (1.54)
  waiting for transfers between devices: 282 us -> 527 us
  starting transfers between devices: 16.6 us -> 34 us
  local copies, waits for them, and re-layouts: 56.5 us -> 64.8 us
    all_to_all x0 -> x1, waiting for transfers between devices: none -> 425 us  [_recast_tracks(): jax.lax.all_to_all(jnp.stack(jax.lax.axis_size(mesh_ax) * [arr_in]), mesh...]
    all_gather x1 -> x0, waiting for transfers between devices: 221 us -> none  [on_device(): lax.all_gather(key_value_weight, 'fsdp', axis=0, tiled=True)]
    reduce_scatter x1, waiting for transfers between devices: 58 us -> 100 us  [on_device(): lax.psum_scatter(partial_value.astype(jnp.bfloat16), 'seq', scatter_dimen...]
    all_to_all x0 -> x1, starting transfers between devices: none -> 11.7 us  [_recast_tracks(): jax.lax.all_to_all(jnp.stack(jax.lax.axis_size(mesh_ax) * [arr_in]), mesh...]
    another operation x0 -> x1, local copies, waits for them, and re-layouts: none -> 8.34 us  [_recast_tracks(): jnp.stack(jax.lax.axis_size(mesh_ax) * [arr_in])]
    unnamed x33 -> x31, local copies, waits for them, and re-layouts: 27.8 us -> 27.8 us
  transfers between devices with their start and end apart: 5 -> 5, of which waited for: 3 -> 3; matrix products, arithmetic and copies ran while one was open for 19% -> 12% of each run, Pallas kernels for 0% -> 0%
where the time goes in v1:
time: 770 us; the launch traced here: 764 us
  waiting for transfers between devices  527 us (68%)
  other arithmetic  71.4 us (9%)
  local copies, waits for them, and re-layouts  64.8 us (8%)
  starting transfers between devices  34 us (4%)
  matrix products  29.2 us (4%)
  blocking collectives  20.7 us (3%)
  between operations  14.6 us (2%)
    all_to_all x1, waiting for transfers between devices, _recast_tracks(): jax.lax.all_to_all(jnp.stack(jax.lax.axis_size(mesh_ax) * [arr_in]), mesh...  425 us
    reduce_scatter x1, waiting for transfers between devices, on_device(): lax.psum_scatter(partial_value.astype(jnp.bfloat16), 'seq', scatter_dimen...  100 us
    unnamed x4, other arithmetic  57.5 us
    unnamed x31, local copies, waits for them, and re-layouts  27.8 us
    all_to_all x1, blocking collectives, on_device(): lax.all_to_all(attn_heads[None], 'seq', split_axis=1, concat_axis=2, tile...  20.7 us
  transfers between devices with their start and end apart: 5, of which 3 were waited for; matrix products, arithmetic and copies ran while one was open for 12% of the time, Pallas kernels for 0%

profile of v1, /device:TPU:8, one launch (start us, length us, event | category | flops | bytes accessed | tf_op | source)
XLA Modules:
  0.0 764.5 jit_solution(11425218029641732076)
XLA Ops:
  7.2 8.3 %stack.2 = bf16[16,320,2048]{2,1,0:T(8,128)(2,1)} broadcast(bf16[320,2048]{1,0:T(8,128)(2,1)} %param.9), dimensions={1,2} | broadcast | bytes 22282240 | tf_op jit(solution)/shard_map/stack | solution.py:13
  15.5 11.7 %all-to-all-start = ((bf16[16,320,2048]{2,1,0:T(8,128)(2,1)}), bf16[16,320,2048]{2,1,0:T(8,128)(2,1)}, u32[]{:S(2)}, u32[]{:S(2)}) async-start(bf16[16,320,2048]{2,1,0:T(8,128)(2,1)} %stack.2), calls=%async_computation | async-start | bytes 41943040 | tf_op jit(solution)/shard_map/all_to_all | solution.py:13
  27.6 5.0 copy.69
  33.2 23.3 %reduce.18 = bf16[4096,128]{1,0:T(8,128)(2,1)} reduce(bf16[4096,1,128]{2,1,0:T(2,128)(2,1)S(1)} %bitcast.130, bf16[]{:T(256)} %broadcast.97), dimensions={1}, to_apply=%bitcast.92.reduce_sub_computation | reduce | bytes 2097154
  58.6 425.4 %all-to-all-done = bf16[16,320,2048]{2,1,0:T(8,128)(2,1)} async-done(((bf16[16,320,2048]{2,1,0:T(8,128)(2,1)}), bf16[16,320,2048]{2,1,0:T(8,128)(2,1)}, u32[]{:S(2)}, u32[]{:S(2)}) %all-to-all-start) | async-done | bytes 20971552 | tf_op jit(solution)/shard_map/all_to_all | solution.py:13
  484.0 10.2 %all-to-all-start.3 = ((bf16[16,2,16384]{2,1,0:T(2,128)(2,1)}), bf16[16,2,16384]{2,1,0:T(2,128)(2,1)S(1)}, u32[]{:S(2)}, u32[]{:S(2)}) async-start(bf16[16,2,16384]{2,1,0:T(2,128)(2,1)} %reshape.218), calls=%async_computation.3 | async-start | bytes 2097152 | tf_op jit(solution)/shard_map/all_to_all | solution.py:79
  494.5 8.5 %fusion.19 = f32[128,2048]{1,0:T(8,128)S(1)} fusion(bf16[5120,2048]{1,0:T(8,128)(2,1)} %bitcast.13, bf16[1,128,5120]{2,1,0:T(8,128)(2,1)S(1)} %copy-done), kind=kOutput, calls=%fused_computation.25 | convolution fusion | flops 2684354560 | bytes 23330816 | tf_op jit(solution)/shard_map/dot_general | solution.py:58
  503.9 8.1 %copy.93 = bf16[1,128,2048]{1,0,2:T(2,128)(2,1)S(1)} copy(bf16[1,128,2048]{1,2,0:T(8,128)(2,1)S(1)} %bitcast.140) | data formatting | bytes 1048576 | tf_op jit(solution)/shard_map/reshape | solution.py:74
  512.1 12.2 %reduce.17 = bf16[2048,128]{1,0:T(8,128)(2,1)} reduce(bf16[2048,1,128]{2,1,0:T(2,128)(2,1)S(1)} %bitcast.138, bf16[]{:T(256)} %broadcast.97), dimensions={1}, to_apply=%bitcast.106.reduce_sub_computation | reduce | bytes 1048578
  526.3 6.0 all-to-all-start.2
  532.7 8.1 %copy.94 = bf16[1,128,2048]{1,0,2:T(2,128)(2,1)S(1)} copy(bf16[1,128,2048]{1,2,0:T(8,128)(2,1)S(1)} %bitcast.141) | data formatting | bytes 1048576 | tf_op jit(solution)/shard_map/reshape | solution.py:77
  540.8 11.5 %reduce.16 = bf16[2048,128]{1,0:T(8,128)(2,1)S(1)} reduce(bf16[2048,1,128]{2,1,0:T(2,128)(2,1)S(1)} %bitcast.139, bf16[]{:T(256)} %broadcast.97), dimensions={1}, to_apply=%bitcast.107.reduce_sub_computation | reduce | bytes 1048578
  553.2 5.9 all-to-all-start.1
  559.4 4.3 reshape.219
  573.3 37.5 %while.14 = (s32[]{:T(128)}, bf16[4,512,256]{2,1,0:T(8,128)(2,1)S(1)}, s32[4]{0:T(128)S(1)}, bf16[2048,1,128]{2,0,1:T(8,128)(2,1)}, s32[2048]{0:T(1024)S(1)}, /*...) while((s32[]{:T(128)}, ...), condition=%wide.region_6.7_spmd, body=%wide.region_3.6_spmd.sunk | while | flops 829816832 | bytes 26538244 | solution.py:116
  575.9 2.5 fusion.40
  585.2 2.5 fusion.40
  594.6 2.5 fusion.40
  604.0 2.5 fusion.40
  611.8 3.2 copy.92
  615.0 10.5 %reduce.19 = bf16[2048,256]{1,0:T(8,128)(2,1)S(1)} reduce(bf16[2048,1,256]{2,1,0:T(2,128)(2,1)S(1)} %bitcast.131, bf16[]{:T(256)} %broadcast.97), dimensions={1}, to_apply=%bitcast.105.reduce_sub_computation | reduce | bytes 2097154
  625.8 20.7 %all_to_all.68 = bf16[16,2,16384]{2,1,0:T(2,128)(2,1)} all-to-all(bf16[16,2,16384]{2,1,0:T(2,128)(2,1)S(1)} %reshape.220), channel_id=1, replica_groups=mesh['fsdp'=16,'seq'=16] {'seq'}, dimensions={0} | all-to-all | bytes 2097152 | tf_op jit(solution)/shard_map/all_to_all | solution.py:119
  646.5 4.3 reshape.221
  656.0 100.0 %reduce-scatter.2.cloned.1.call-done = bf16[16,256]{1,0:T(8,128)(2,1)} async-done(((bf16[16,4096]{1,0:T(8,128)(2,1)}), bf16[16,256]{1,0:T(8,128)(2,1)}) %reduce-scatter.2.cloned.1.call-update) | async-done | bytes 8208 | tf_op jit(solution)/shard_map/reduce_scatter | solution.py:126
  (107 shorter events, 49.7 us)
Async XLA Ops:
  7.2 487.3 %copy-start = (bf16[1,128,5120]{2,1,0:T(8,128)(2,1)S(1)}, bf16[1,128,5120]{2,1,0:T(8,128)(2,1)}, u32[]{:S(2)}) copy-start(bf16[1,128,5120]{2,1,0:T(8,128)(2,1)} %param.7) | copy-start | bytes 3932164
  15.5 11.7 %copy-start.6 = (s32[1,16]{1,0:T(1,128)S(1)}, s32[1,16]{1,0:T(1,128)}, u32[]{:S(2)}) copy-start(s32[1,16]{1,0:T(1,128)} %param.10) | copy-start | bytes 196
  15.5 11.9 %copy-start.7 = (s32[1,16]{1,0:T(1,128)S(1)}, s32[1,16]{1,0:T(1,128)}, u32[]{:S(2)}) copy-start(s32[1,16]{1,0:T(1,128)} %param.11) | copy-start | bytes 196
  15.5 468.4 %all-to-all-start = ((bf16[16,320,2048]{2,1,0:T(8,128)(2,1)}), bf16[16,320,2048]{2,1,0:T(8,128)(2,1)}, u32[]{:S(2)}, u32[]{:S(2)}) async-start(bf16[16,320,2048]{2,1,0:T(8,128)(2,1)} %stack.2), calls=%async_computation | async-start | bytes 41943040 | tf_op jit(solution)/shard_map/all_to_all | solution.py:13
  484.0 42.3 %all-to-all-start.3 = ((bf16[16,2,16384]{2,1,0:T(2,128)(2,1)}), bf16[16,2,16384]{2,1,0:T(2,128)(2,1)S(1)}, u32[]{:S(2)}, u32[]{:S(2)}) async-start(bf16[16,2,16384]{2,1,0:T(2,128)(2,1)} %reshape.218), calls=%async_computation.3 | async-start | bytes 2097152 | tf_op jit(solution)/shard_map/all_to_all | solution.py:79
  526.3 33.1 %copy-start.2 = (bf16[16,2,16384]{2,1,0:T(2,128)(2,1)}, bf16[16,2,16384]{2,1,0:T(2,128)(2,1)S(1)}, u32[]{:S(2)}) copy-start(bf16[16,2,16384]{2,1,0:T(2,128)(2,1)S(1)} %all-to-all-done.3) | copy-start | bytes 3145732
  526.3 26.9 %all-to-all-start.2 = ((bf16[16,2,8192]{2,1,0:T(2,128)(2,1)}), bf16[16,2,8192]{2,1,0:T(2,128)(2,1)}, u32[]{:S(2)}, u32[]{:S(2)}) async-start(bf16[16,2,8192]{2,1,0:T(2,128)(2,1)} %reshape.216), calls=%async_computation.2 | async-start | bytes 1048576 | tf_op jit(solution)/shard_map/all_to_all | solution.py:80
  553.2 16.7 %all-to-all-start.1 = ((bf16[16,2,8192]{2,1,0:T(2,128)(2,1)}), bf16[16,2,8192]{2,1,0:T(2,128)(2,1)}, u32[]{:S(2)}, u32[]{:S(2)}) async-start(bf16[16,2,8192]{2,1,0:T(2,128)(2,1)} %reshape.214), calls=%async_computation.1 | async-start | bytes 1048576 | tf_op jit(solution)/shard_map/all_to_all | solution.py:81
  559.1 196.9 %reduce-scatter.2.cloned.1.call-start = ((), (), s32[]{:S(2)}) async-start(), calls=%async_computation.6 | async-start | bytes 139264 | tf_op jit(solution)/shard_map/reduce_scatter | solution.py:126
  563.9 9.4 %copy-start.3 = (bf16[4,512,256]{2,1,0:T(8,128)(2,1)S(1)}, bf16[4,512,256]{2,1,0:T(8,128)(2,1)}, u32[]{:S(2)}) copy-start(bf16[4,512,256]{2,1,0:T(8,128)(2,1)} %custom-call) | copy-start | bytes 3145732
  575.8 4.2 copy-start.5
  585.2 4.2 copy-start.5
  594.6 4.2 copy-start.5
  604.0 4.2 copy-start.5
  610.8 1.0 copy-start.4
  625.8 131.6 %copy-start.1 = (bf16[1,128,5120]{2,1,0:T(8,128)(2,1)S(1)}, bf16[1,128,5120]{2,1,0:T(8,128)(2,1)}, u32[]{:S(2)}) copy-start(bf16[1,128,5120]{2,1,0:T(8,128)(2,1)} %param.7) | copy-start | bytes 3932164
Sparse Core Ops, SparseCore 0:
  654.8 101.1 reduce-scatter.1
